TPU v7x, 512 devices: a whole 4x4x16 slice. The times are simulated.
512 devices in a mesh: loop: 64 (over z_lo, x, core), rep: 8 (over y, z_hi).
Axes of the slice: x: 4, y: 4, z: 16 (z_hi: 2, z_lo: 8; z = z_hi * 8 + z_lo), core: 2. Of those that a mesh axis runs over, the one named last changes fastest.
Arguments:
- features: bfloat16 [65536, 256], P(('loop', 'rep')), may hold values from -6 to 6
- weight: bfloat16 [256, 256], replicated, may hold values from -0.375 to 0.375
- tile_values: bfloat16 [49152, 128, 128], P(('loop', 'rep')), may hold values from -0.375 to 0.375
- tile_coords: int32 [49152, 2], P(('loop', 'rep')), may hold values from 0 to 7
- tile_counts: int32 [512, 8], P(('loop', 'rep')), may hold values from 1 to 12, as said below
Outputs:
- activated: bfloat16 [65536, 256], P(('loop', 'rep'))
Inputs may be any that keep to these rules, and one draw needn't show every extreme that they name: `tile_counts`: some list uses all 12 slots at some step; loads differ strongly between lists. `tile_coords`: row block within the group's rows and column block within the slab of that step.
All inputs are finite; a program needn't handle non-finite values.
Results may differ from a plain program's by a relative error of at most 0.0049.
Values may be sent and summed in bfloat16 or wider, within the bound.
A program may use at most 64 MiB of HBM per device.

v0:
```python
import jax
import jax.numpy as jnp
from jax import lax
from jax.sharding import PartitionSpec as P


def from_behind(x, axis, by):
    count = lax.axis_size(axis)
    return lax.ppermute(x, axis, [(i, (i + by) % count) for i in range(count)])


def local(features, weight, tile_values, tile_coords, tile_counts):
    rep_size = lax.axis_size("rep")
    loop_size = lax.axis_size("loop")
    step_count = loop_size // rep_size
    tile_size = tile_values.shape[1]
    feat_width = features.shape[1]
    slot_count = tile_values.shape[0] // step_count
    current_slab = lax.all_gather(features, "rep", axis=0, tiled=True)
    block_count = current_slab.shape[0] // tile_size
    values = tile_values.reshape(step_count, slot_count, tile_size, tile_size)
    coords = tile_coords.reshape(step_count, slot_count, 2)
    counts = tile_counts.reshape(step_count)
    rep_rank = lax.axis_index("rep")
    for bit_index in range(rep_size.bit_length() - 1):
        shifted = from_behind(current_slab, "loop", step_count * (1 << bit_index))
        current_slab = jnp.where(rep_rank >> bit_index & 1 == 1, shifted, current_slab)
    running = jnp.zeros((block_count, tile_size, feat_width), jnp.float32)
    for step_index in range(step_count):
        slab_blocks = current_slab.reshape(block_count, tile_size, feat_width)
        pieces = jnp.take(slab_blocks, coords[step_index, :, 1], axis=0)
        products = jnp.einsum(
            "ktc,kcf->ktf", values[step_index], pieces, preferred_element_type=jnp.float32
        )
        live_slot = (jnp.arange(slot_count) < counts[step_index]).astype(jnp.float32)
        running = running.at[coords[step_index, :, 0]].add(products * live_slot[:, None, None])
        if step_index + 1 < step_count:
            current_slab = from_behind(current_slab, "loop", 1)
    summed = lax.psum_scatter(
        running.reshape(block_count * tile_size, feat_width), "rep", scatter_dimension=0, tiled=True
    )
    aggregated = summed.astype(jnp.bfloat16)
    product = jnp.dot(aggregated, weight, preferred_element_type=jnp.float32)
    return jnp.maximum(product, 0.0).astype(jnp.bfloat16)


def solution(mesh):
    placed = (
        P(("loop", "rep"), None),
        P(),
        P(("loop", "rep"), None, None),
        P(("loop", "rep"), None),
        P(("loop", "rep"), None),
    )
    return jax.shard_map(
        local, mesh=mesh, in_specs=placed, out_specs=P(("loop", "rep"), None), check_vma=False
    )
```

profile of v0, /device:TPU:2, one launch (start us, length us, event | category | flops | bytes accessed | tf_op | source)
XLA Modules:
  0.0 455.2 jit_solution(15041202940088888313)
XLA Ops:
  6.5 90.3 %all_gather.3 = bf16[1024,256]{1,0:T(8,128)(2,1)S(1)} all-gather(bf16[128,256]{1,0:T(8,128)(2,1)} %param.7), channel_id=1, replica_groups=mesh['loop'=64,'rep'=8] {'rep'}, dimensions={0}, use_global_device_ids=true | all-gather | bytes 589824 | tf_op jit(solution)/shard_map/all_gather | solution.py:19
  96.8 6.3 %collective-permute-start = (bf16[1024,256]{1,0:T(8,128)(2,1)S(1)}, bf16[1024,256]{1,0:T(8,128)(2,1)S(1)}, u32[]{:S(2)}, u32[]{:S(2)}) collective-permute-start(bf16[1024,256]{1,0:T(8,128)(2,1)S(1)} %all_gather.3), channel_id=1, source_target_pairs={{0,64},{8,72},{16,80},{24,88},{32,96},{40,104},{48,112},{56,120},{... | collective-permute-start | bytes 1572872 | tf_op jit(solution)/shard_map/ppermute | solution.py:9
  103.2 12.8 %collective-permute-done = bf16[1024,256]{1,0:T(8,128)(2,1)S(1)} collective-permute-done((bf16[1024,256]{1,0:T(8,128)(2,1)S(1)}, bf16[1024,256]{1,0:T(8,128)(2,1)S(1)}, u32[]{:S(2)}, u32[]{:S(2)}) %collective-permute-start) | collective-permute-done | bytes 524320 | tf_op jit(solution)/shard_map/ppermute | solution.py:9
  116.0 5.9 %collective-permute-start.1 = (bf16[1024,256]{1,0:T(8,128)(2,1)S(1)}, bf16[1024,256]{1,0:T(8,128)(2,1)S(1)}, u32[]{:S(2)}, u32[]{:S(2)}) collective-permute-start(bf16[1024,256]{1,0:T(8,128)(2,1)S(1)} %broadcast_select_fusion), channel_id=1, source_target_pairs={{0,128},{8,136},{16,144},{24,152},{32,160},{40,168},{48,176},{56,1... | collective-permute-start | bytes 1572872 | tf_op jit(solution)/shard_map/ppermute | solution.py:9
  122.0 28.9 %collective-permute-done.1 = bf16[1024,256]{1,0:T(8,128)(2,1)S(1)} collective-permute-done((bf16[1024,256]{1,0:T(8,128)(2,1)S(1)}, bf16[1024,256]{1,0:T(8,128)(2,1)S(1)}, u32[]{:S(2)}, u32[]{:S(2)}) %collective-permute-start.1) | collective-permute-done | bytes 524320 | tf_op jit(solution)/shard_map/ppermute | solution.py:9
  150.9 2.7 collective-permute-start.2
  153.7 0.7 fusion.50
  154.4 0.6 compare_convert_fusion.7
  155.0 1.2 compare_convert_fusion.6
  156.2 16.9 %collective-permute-done.2 = bf16[1024,256]{1,0:T(8,128)(2,1)S(1)} collective-permute-done((bf16[1024,256]{1,0:T(8,128)(2,1)S(1)}, bf16[1024,256]{1,0:T(8,128)(2,1)S(1)}, u32[]{:S(2)}, u32[]{:S(2)}) %collective-permute-start.2) | collective-permute-done | bytes 524320 | tf_op jit(solution)/shard_map/ppermute | solution.py:9
  173.2 1.9 collective-permute-start.3
  175.1 1.2 compare_convert_fusion.5
  176.3 1.1 compare_convert_fusion.4
  177.4 1.2 compare_convert_fusion.3
  179.3 6.8 %collective-permute-done.3 = bf16[1024,256]{1,0:T(8,128)(2,1)S(1)} collective-permute-done((bf16[1024,256]{1,0:T(8,128)(2,1)S(1)}, bf16[1024,256]{1,0:T(8,128)(2,1)S(1)}, u32[]{:S(2)}, u32[]{:S(2)}) %collective-permute-start.3) | collective-permute-done | bytes 524320 | tf_op jit(solution)/shard_map/ppermute | solution.py:9
  186.1 1.9 collective-permute-start.4
  188.0 1.2 compare_convert_fusion.2
  191.0 5.6 %collective-permute-done.4 = bf16[1024,256]{1,0:T(8,128)(2,1)S(1)} collective-permute-done((bf16[1024,256]{1,0:T(8,128)(2,1)S(1)}, bf16[1024,256]{1,0:T(8,128)(2,1)S(1)}, u32[]{:S(2)}, u32[]{:S(2)}) %collective-permute-start.4) | collective-permute-done | bytes 524320 | tf_op jit(solution)/shard_map/ppermute | solution.py:9
  196.6 1.9 collective-permute-start.5
  198.5 1.1 compare_convert_fusion.1
  199.6 12.5 %collective-permute-done.5 = bf16[1024,256]{1,0:T(8,128)(2,1)} collective-permute-done((bf16[1024,256]{1,0:T(8,128)(2,1)S(1)}, bf16[1024,256]{1,0:T(8,128)(2,1)}, u32[]{:S(2)}, u32[]{:S(2)}) %collective-permute-start.5) | collective-permute-done | bytes 524320 | tf_op jit(solution)/shard_map/ppermute | solution.py:9
  212.1 1.9 collective-permute-start.6
  214.0 1.1 compare_convert_fusion
  216.4 2.6 multiply_bitcast_fusion.7
  219.0 1.9 copy.33
  221.0 1.8 scatter_fusion
  222.8 1.8 gather_fusion.1
  224.6 7.1 %collective-permute-done.6 = bf16[1024,256]{1,0:T(8,128)(2,1)} collective-permute-done((bf16[1024,256]{1,0:T(8,128)(2,1)}, bf16[1024,256]{1,0:T(8,128)(2,1)}, u32[]{:S(2)}, u32[]{:S(2)}) %collective-permute-start.6) | collective-permute-done | bytes 524320 | tf_op jit(solution)/shard_map/ppermute | solution.py:9
  231.7 1.9 collective-permute-start.7
  233.6 1.5 multiply_bitcast_fusion.6
  235.1 1.6 copy.37
  236.7 3.1 scatter_fusion.1
  239.8 0.7 gather_fusion.2
  240.6 1.5 multiply_bitcast_fusion.5
  242.1 1.6 copy.41
  243.7 3.1 scatter_fusion.2
  246.8 1.8 gather_fusion.3
  248.6 2.6 collective-permute-done.7
  251.2 2.1 collective-permute-start.8
  253.3 1.5 multiply_bitcast_fusion.4
  254.8 1.6 copy.45
  256.4 3.1 scatter_fusion.3
  259.5 1.6 gather_fusion.4
  261.2 1.5 multiply_bitcast_fusion.3
  262.7 1.6 copy.49
  264.3 3.1 scatter_fusion.4
  267.4 1.6 gather_fusion.5
  269.1 1.6 collective-permute-done.8
  270.7 1.9 collective-permute-start.9
  272.6 1.5 multiply_bitcast_fusion.2
  274.1 1.6 copy.53
  275.7 3.1 scatter_fusion.5
  278.9 1.6 gather_fusion.6
  280.6 1.5 multiply_bitcast_fusion.1
  282.1 1.6 copy.57
  283.7 3.1 scatter_fusion.6
  286.8 3.4 collective-permute-done.9
  290.2 1.6 gather_fusion.7
  291.9 2.6 multiply_bitcast_fusion
  294.5 1.9 copy.61
  296.4 1.8 scatter_fusion.7
  298.3 1.0 copy-done.1
  299.2 147.4 %reduce-scatter.2.cloned.1.call-done = f32[128,256]{1,0:T(8,128)} async-done(((f32[1024,256]{1,0:T(8,128)}), f32[128,256]{1,0:T(8,128)}) %reduce-scatter.2.cloned.1.call-update) | async-done | bytes 131088 | tf_op jit(solution)/shard_map/reduce_scatter | solution.py:39
  446.7 1.7 fusion
  (55 shorter events, 4.0 us)
Async XLA Ops:
  6.5 440.1 %copy-start = (bf16[256,256]{1,0:T(8,128)(2,1)S(1)}, bf16[256,256]{1,0:T(8,128)(2,1)}, u32[]{:S(2)}) copy-start(bf16[256,256]{1,0:T(8,128)(2,1)} %param.8) | copy-start | bytes 393220
  6.5 440.1 %reduce-scatter.2.cloned.1.call-start = ((), (), s32[]{:S(2)}) async-start(), calls=%async_computation.1 | async-start | bytes 1179648 | tf_op jit(solution)/shard_map/reduce_scatter | solution.py:39
  96.8 19.1 %collective-permute-start = (bf16[1024,256]{1,0:T(8,128)(2,1)S(1)}, bf16[1024,256]{1,0:T(8,128)(2,1)S(1)}, u32[]{:S(2)}, u32[]{:S(2)}) collective-permute-start(bf16[1024,256]{1,0:T(8,128)(2,1)S(1)} %all_gather.3), channel_id=1, source_target_pairs={{0,64},{8,72},{16,80},{24,88},{32,96},{40,104},{48,112},{56,120},{... | collective-permute-start | bytes 1572872 | tf_op jit(solution)/shard_map/ppermute | solution.py:9
  103.1 50.5 %copy-start.16 = (s32[96,2]{0,1:T(2,128)S(1)}, s32[96,2]{0,1:T(2,128)}, u32[]{:S(2)}) copy-start(s32[96,2]{0,1:T(2,128)} %param.10) | copy-start | bytes 2308
  103.2 50.5 %copy-start.5 = (s32[1,8]{1,0:T(1,128)S(1)}, s32[1,8]{1,0:T(1,128)}, u32[]{:S(2)}) copy-start(s32[1,8]{1,0:T(1,128)} %param.11) | copy-start | bytes 100
  116.0 34.8 %collective-permute-start.1 = (bf16[1024,256]{1,0:T(8,128)(2,1)S(1)}, bf16[1024,256]{1,0:T(8,128)(2,1)S(1)}, u32[]{:S(2)}, u32[]{:S(2)}) collective-permute-start(bf16[1024,256]{1,0:T(8,128)(2,1)S(1)} %broadcast_select_fusion), channel_id=1, source_target_pairs={{0,128},{8,136},{16,144},{24,152},{32,160},{40,168},{48,176},{56,1... | collective-permute-start | bytes 1572872 | tf_op jit(solution)/shard_map/ppermute | solution.py:9
  150.9 22.2 %collective-permute-start.2 = (bf16[1024,256]{1,0:T(8,128)(2,1)S(1)}, bf16[1024,256]{1,0:T(8,128)(2,1)S(1)}, u32[]{:S(2)}, u32[]{:S(2)}) collective-permute-start(bf16[1024,256]{1,0:T(8,128)(2,1)S(1)} %broadcast_select_fusion.1), channel_id=1, source_target_pairs={{0,256},{8,264},{16,272},{24,280},{32,288},{40,296},{48,304},{56,3... | collective-permute-start | bytes 1572872 | tf_op jit(solution)/shard_map/ppermute | solution.py:9
  173.2 12.9 %collective-permute-start.3 = (bf16[1024,256]{1,0:T(8,128)(2,1)S(1)}, bf16[1024,256]{1,0:T(8,128)(2,1)S(1)}, u32[]{:S(2)}, u32[]{:S(2)}) collective-permute-start(bf16[1024,256]{1,0:T(8,128)(2,1)S(1)} %broadcast_select_fusion.2), channel_id=1, source_target_pairs={{0,8},{8,16},{16,24},{24,32},{32,40},{40,48},{48,56},{56,64},{64,7... | collective-permute-start | bytes 1572872 | tf_op jit(solution)/shard_map/ppermute | solution.py:9
  186.1 32.9 %copy-start.2 = (bf16[1024,256]{1,0:T(8,128)(2,1)}, bf16[1024,256]{1,0:T(8,128)(2,1)S(1)}, u32[]{:S(2)}) copy-start(bf16[1024,256]{1,0:T(8,128)(2,1)S(1)} %collective-permute-done.3) | copy-start | bytes 1572868
  186.1 10.5 %collective-permute-start.4 = (bf16[1024,256]{1,0:T(8,128)(2,1)S(1)}, bf16[1024,256]{1,0:T(8,128)(2,1)S(1)}, u32[]{:S(2)}, u32[]{:S(2)}) collective-permute-start(bf16[1024,256]{1,0:T(8,128)(2,1)S(1)} %collective-permute-done.3), channel_id=1, source_target_pairs={{0,8},{8,16},{16,24},{24,32},{32,40},{40,48},{48,56},{56,64},{64,7... | collective-permute-start | bytes 1572872 | tf_op jit(solution)/shard_map/ppermute | solution.py:9
  196.5 19.2 %copy-start.3 = (bf16[1024,256]{1,0:T(8,128)(2,1)}, bf16[1024,256]{1,0:T(8,128)(2,1)S(1)}, u32[]{:S(2)}) copy-start(bf16[1024,256]{1,0:T(8,128)(2,1)S(1)} %collective-permute-done.4) | copy-start | bytes 1572868
  196.6 15.6 %collective-permute-start.5 = (bf16[1024,256]{1,0:T(8,128)(2,1)S(1)}, bf16[1024,256]{1,0:T(8,128)(2,1)}, u32[]{:S(2)}, u32[]{:S(2)}) collective-permute-start(bf16[1024,256]{1,0:T(8,128)(2,1)S(1)} %collective-permute-done.4), channel_id=1, source_target_pairs={{0,8},{8,16},{16,24},{24,32},{32,40},{40,48},{48,56},{56,64},{64,7... | collective-permute-start | bytes 1572872 | tf_op jit(solution)/shard_map/ppermute | solution.py:9
  212.1 19.5 %collective-permute-start.6 = (bf16[1024,256]{1,0:T(8,128)(2,1)}, bf16[1024,256]{1,0:T(8,128)(2,1)}, u32[]{:S(2)}, u32[]{:S(2)}) collective-permute-start(bf16[1024,256]{1,0:T(8,128)(2,1)} %collective-permute-done.5), channel_id=1, source_target_pairs={{0,8},{8,16},{16,24},{24,32},{32,40},{40,48},{48,56},{56,64},{64,7... | collective-permute-start | bytes 1572872 | tf_op jit(solution)/shard_map/ppermute | solution.py:9
  231.7 19.5 %collective-permute-start.7 = (bf16[1024,256]{1,0:T(8,128)(2,1)}, bf16[1024,256]{1,0:T(8,128)(2,1)}, u32[]{:S(2)}, u32[]{:S(2)}) collective-permute-start(bf16[1024,256]{1,0:T(8,128)(2,1)} %collective-permute-done.6), channel_id=1, source_target_pairs={{0,8},{8,16},{16,24},{24,32},{32,40},{40,48},{48,56},{56,64},{64,7... | collective-permute-start | bytes 1572872 | tf_op jit(solution)/shard_map/ppermute | solution.py:9
  235.1 1.6 copy-start.15
  236.7 3.1 copy-start.4
  242.1 1.6 copy-start.14
  251.2 19.5 %collective-permute-start.8 = (bf16[1024,256]{1,0:T(8,128)(2,1)}, bf16[1024,256]{1,0:T(8,128)(2,1)}, u32[]{:S(2)}, u32[]{:S(2)}) collective-permute-start(bf16[1024,256]{1,0:T(8,128)(2,1)} %collective-permute-done.7), channel_id=1, source_target_pairs={{0,8},{8,16},{16,24},{24,32},{32,40},{40,48},{48,56},{56,64},{64,7... | collective-permute-start | bytes 1572872 | tf_op jit(solution)/shard_map/ppermute | solution.py:9
  254.8 1.6 copy-start.13
  262.7 1.6 copy-start.12
  267.4 5.2 %copy-start.8 = (pred[12]{0:T(512)(128)(4,1)S(1)}, pred[12]{0:T(512)(128)(4,1)}, u32[]{:S(2)}) copy-start(pred[12]{0:T(512)(128)(4,1)} %get-tuple-element.24) | copy-start | bytes 40
  270.7 19.5 %collective-permute-start.9 = (bf16[1024,256]{1,0:T(8,128)(2,1)}, bf16[1024,256]{1,0:T(8,128)(2,1)}, u32[]{:S(2)}, u32[]{:S(2)}) collective-permute-start(bf16[1024,256]{1,0:T(8,128)(2,1)} %collective-permute-done.8), channel_id=1, source_target_pairs={{0,8},{8,16},{16,24},{24,32},{32,40},{40,48},{48,56},{56,64},{64,7... | collective-permute-start | bytes 1572872 | tf_op jit(solution)/shard_map/ppermute | solution.py:9
  274.1 1.6 copy-start.11
  278.9 1.7 copy-start.7
  278.9 1.7 copy-start.17
  282.1 1.6 copy-start.10
  286.8 5.0 %copy-start.6 = (pred[12]{0:T(512)(128)(4,1)S(1)}, pred[12]{0:T(512)(128)(4,1)}, u32[]{:S(2)}) copy-start(pred[12]{0:T(512)(128)(4,1)} %get-tuple-element.6) | copy-start | bytes 40
  286.8 5.0 %copy-start.18 = (f32[12]{0:T(128)S(1)}, f32[12]{0:T(128)}, u32[]{:S(2)}) copy-start(f32[12]{0:T(128)} %compare_convert_fusion) | copy-start | bytes 148
  294.5 1.9 copy-start.9
  298.3 1.0 copy-start.1
Sparse Core Ops, SparseCore 0:
  299.4 147.2 reduce-scatter.1
where the time goes:
time: 456 us; the launch traced here: 455 us
  waiting for transfers between devices  246 us (54%)
  blocking collectives  90.3 us (20%)
  other arithmetic  34.3 us (8%)
  starting transfers between devices  28.5 us (6%)
  local copies, waits for them, and re-layouts  26.7 us (6%)
  matrix products  15.9 us (3%)
  between operations  13.9 us (3%)
    reduce_scatter x1, waiting for transfers between devices, local(): lax.psum_scatter(running.reshape(block_count * tile_size, feat_width), 'r...  147 us
    ppermute x10, waiting for transfers between devices, from_behind(): return lax.ppermute(x, axis, [(i, (i + by) % count) for i in range(count)])  98.2 us
    all_gather x1, blocking collectives, local(): current_slab = lax.all_gather(features, 'rep', axis=0, tiled=True)  90.3 us
    ppermute x10, starting transfers between devices, from_behind(): return lax.ppermute(x, axis, [(i, (i + by) % count) for i in range(count)])  28.5 us
    scatter-add x8, other arithmetic, local(): running.at[coords[step_index, :, 0]]  22.4 us
    dot_general x8, matrix products, local(): jnp.einsum('ktc,kcf->ktf', values[step_index], pieces, preferred_element_...  14.2 us
    mul x8, local copies, waits for them, and re-layouts, local(): products * live_slot[:, None, None]  13.5 us
    gather x8, local copies, waits for them, and re-layouts, local(): pieces = jnp.take(slab_blocks, coords[step_index, :, 1], axis=0)  11.4 us
  transfers between devices with their start and end apart: 11, of which 11 were waited for; matrix products, arithmetic and copies ran while one was open for 15% of the time, Pallas kernels for 0%

commit v1 on v0

--- a/solution.py
+++ b/solution.py
@@ -16,7 +16,8 @@
     tile_size = tile_values.shape[1]
     feat_width = features.shape[1]
     slot_count = tile_values.shape[0] // step_count
-    current_slab = lax.all_gather(features, "rep", axis=0, tiled=True)
+    stack = jnp.stack([features] * lax.axis_size("rep"))
+    current_slab = jnp.concatenate(lax.all_to_all(stack, "rep", 0, 0), axis=0)
     block_count = current_slab.shape[0] // tile_size
     values = tile_values.reshape(step_count, slot_count, tile_size, tile_size)
     coords = tile_coords.reshape(step_count, slot_count, 2)

time: 456 us -> 418 us (0.917)
  the two profiles are of different devices: /device:TPU:2 before, /device:TPU:6 now
where the time goes in v1:
time: 418 us; the launch traced here: 416 us
  waiting for transfers between devices  242 us (58%)
  starting transfers between devices  45.8 us (11%)
  blocking collectives  36.8 us (9%)
  other arithmetic  34.4 us (8%)
  local copies, waits for them, and re-layouts  27.6 us (7%)
  matrix products  15.9 us (4%)
  between operations  14 us (3%)
    reduce_scatter x1, waiting for transfers between devices, local(): lax.psum_scatter(running.reshape(block_count * tile_size, feat_width), 'r...  147 us
    ppermute x10, waiting for transfers between devices, from_behind(): return lax.ppermute(x, axis, [(i, (i + by) % count) for i in range(count)])  95 us
    ppermute x10, starting transfers between devices, from_behind(): return lax.ppermute(x, axis, [(i, (i + by) % count) for i in range(count)])  45.8 us
    all_to_all x1, blocking collectives, local(): current_slab = jnp.concatenate(lax.all_to_all(stack, 'rep', 0, 0), axis=0)  36.8 us
    scatter-add x8, other arithmetic, local(): running.at[coords[step_index, :, 0]]  22.4 us
    dot_general x8, matrix products, local(): jnp.einsum('ktc,kcf->ktf', values[step_index], pieces, preferred_element_...  14.2 us
    mul x8, local copies, waits for them, and re-layouts, local(): products * live_slot[:, None, None]  13.5 us
    gather x8, local copies, waits for them, and re-layouts, local(): pieces = jnp.take(slab_blocks, coords[step_index, :, 1], axis=0)  11.4 us
  transfers between devices with their start and end apart: 11, of which 7 were waited for; matrix products, arithmetic and copies ran while one was open for 16% of the time, Pallas kernels for 0%

profile of v1, /device:TPU:6, one launch (start us, length us, event | category | flops | bytes accessed | tf_op | source)
XLA Modules:
  0.0 416.3 jit_solution(17111508761935468788)
XLA Ops:
  6.5 0.9 stack.2
  7.5 36.8 %all_to_all.5 = bf16[8,128,256]{2,1,0:T(8,128)(2,1)S(1)} all-to-all(bf16[8,128,256]{2,1,0:T(8,128)(2,1)S(1)} %stack.2), channel_id=1, replica_groups=mesh['loop'=64,'rep'=8] {'rep'}, dimensions={0} | all-to-all | bytes 1048576 | tf_op jit(solution)/shard_map/all_to_all | solution.py:20
  44.3 19.4 %collective-permute-start = (bf16[1024,256]{1,0:T(8,128)(2,1)S(1)}, bf16[1024,256]{1,0:T(8,128)(2,1)S(1)}, u32[]{:S(2)}, u32[]{:S(2)}) collective-permute-start(bf16[1024,256]{1,0:T(8,128)(2,1)S(1)} %bitcast.160), channel_id=1, source_target_pairs={{0,64},{8,72},{16,80},{24,88},{32,96},{40,104},{48,112},{56,120},{... | collective-permute-start | bytes 1572872 | tf_op jit(solution)/shard_map/ppermute | solution.py:9
  63.7 10.1 %collective-permute-done = bf16[1024,256]{1,0:T(8,128)(2,1)S(1)} collective-permute-done((bf16[1024,256]{1,0:T(8,128)(2,1)S(1)}, bf16[1024,256]{1,0:T(8,128)(2,1)S(1)}, u32[]{:S(2)}, u32[]{:S(2)}) %collective-permute-start) | collective-permute-done | bytes 524320 | tf_op jit(solution)/shard_map/ppermute | solution.py:9
  73.9 4.1 collective-permute-start.1
  78.0 26.5 %collective-permute-done.1 = bf16[1024,256]{1,0:T(8,128)(2,1)S(1)} collective-permute-done((bf16[1024,256]{1,0:T(8,128)(2,1)S(1)}, bf16[1024,256]{1,0:T(8,128)(2,1)S(1)}, u32[]{:S(2)}, u32[]{:S(2)}) %collective-permute-start.1) | collective-permute-done | bytes 524320 | tf_op jit(solution)/shard_map/ppermute | solution.py:9
  104.5 1.9 collective-permute-start.2
  106.6 0.7 fusion.50
  107.3 0.6 compare_convert_fusion.7
  107.9 1.2 compare_convert_fusion.6
  109.1 40.8 %collective-permute-done.2 = bf16[1024,256]{1,0:T(8,128)(2,1)S(1)} collective-permute-done((bf16[1024,256]{1,0:T(8,128)(2,1)S(1)}, bf16[1024,256]{1,0:T(8,128)(2,1)S(1)}, u32[]{:S(2)}, u32[]{:S(2)}) %collective-permute-start.2) | collective-permute-done | bytes 524320 | tf_op jit(solution)/shard_map/ppermute | solution.py:9
  149.9 1.9 collective-permute-start.3
  151.9 1.2 compare_convert_fusion.5
  153.1 1.1 compare_convert_fusion.4
  154.2 1.2 compare_convert_fusion.3
  155.4 0.6 compare_and_fusion
  156.0 4.4 %collective-permute-done.3 = bf16[1024,256]{1,0:T(8,128)(2,1)S(1)} collective-permute-done((bf16[1024,256]{1,0:T(8,128)(2,1)S(1)}, bf16[1024,256]{1,0:T(8,128)(2,1)S(1)}, u32[]{:S(2)}, u32[]{:S(2)}) %collective-permute-start.3) | collective-permute-done | bytes 524320 | tf_op jit(solution)/shard_map/ppermute | solution.py:9
  160.4 1.9 collective-permute-start.4
  162.4 1.2 compare_convert_fusion.2
  163.6 0.6 pad_clamp_fusion.6
  165.3 5.6 %collective-permute-done.4 = bf16[1024,256]{1,0:T(8,128)(2,1)S(1)} collective-permute-done((bf16[1024,256]{1,0:T(8,128)(2,1)S(1)}, bf16[1024,256]{1,0:T(8,128)(2,1)S(1)}, u32[]{:S(2)}, u32[]{:S(2)}) %collective-permute-start.4) | collective-permute-done | bytes 524320 | tf_op jit(solution)/shard_map/ppermute | solution.py:9
  170.9 1.9 collective-permute-start.5
  172.9 1.1 compare_convert_fusion.1
  174.0 7.5 %collective-permute-done.5 = bf16[1024,256]{1,0:T(8,128)(2,1)} collective-permute-done((bf16[1024,256]{1,0:T(8,128)(2,1)S(1)}, bf16[1024,256]{1,0:T(8,128)(2,1)}, u32[]{:S(2)}, u32[]{:S(2)}) %collective-permute-start.5) | collective-permute-done | bytes 524320 | tf_op jit(solution)/shard_map/ppermute | solution.py:9
  181.5 3.6 collective-permute-start.6
  185.1 1.1 compare_convert_fusion
  186.2 0.6 fusion.41
  187.4 2.6 multiply_bitcast_fusion.7
  190.1 1.9 copy.33
  192.0 1.8 scatter_fusion
  193.9 1.8 gather_fusion.1
  195.7 6.6 %collective-permute-start.7 = (bf16[1024,256]{1,0:T(8,128)(2,1)}, bf16[1024,256]{1,0:T(8,128)(2,1)}, u32[]{:S(2)}, u32[]{:S(2)}) collective-permute-start(bf16[1024,256]{1,0:T(8,128)(2,1)} %collective-permute-done.6), channel_id=1, source_target_pairs={{0,8},{8,16},{16,24},{24,32},{32,40},{40,48},{48,56},{56,64},{64,7... | collective-permute-start | bytes 1572872 | tf_op jit(solution)/shard_map/ppermute | solution.py:9
  202.3 1.5 multiply_bitcast_fusion.6
  203.8 1.6 copy.37
  205.4 3.1 scatter_fusion.1
  208.5 0.7 gather_fusion.2
  209.3 1.5 multiply_bitcast_fusion.5
  210.8 1.6 copy.41
  212.4 3.1 scatter_fusion.2
  215.5 1.8 gather_fusion.3
  217.3 2.5 collective-permute-start.8
  219.8 1.5 multiply_bitcast_fusion.4
  221.3 1.6 copy.45
  222.9 3.1 scatter_fusion.3
  226.1 1.6 gather_fusion.4
  227.7 1.5 multiply_bitcast_fusion.3
  229.2 1.6 copy.49
  230.8 3.1 scatter_fusion.4
  234.0 1.6 gather_fusion.5
  235.6 1.9 collective-permute-start.9
  237.6 1.5 multiply_bitcast_fusion.2
  239.1 1.6 copy.53
  240.7 3.1 scatter_fusion.5
  243.9 1.6 gather_fusion.6
  245.5 1.5 multiply_bitcast_fusion.1
  247.0 1.6 copy.57
  248.7 3.1 scatter_fusion.6
  251.8 1.6 gather_fusion.7
  253.5 2.6 multiply_bitcast_fusion
  256.1 1.9 copy.61
  258.0 1.8 scatter_fusion.7
  259.9 1.0 copy-done.1
  260.8 147.0 %reduce-scatter.2.cloned.1.call-done = f32[128,256]{1,0:T(8,128)} async-done(((f32[1024,256]{1,0:T(8,128)}), f32[128,256]{1,0:T(8,128)}) %reduce-scatter.2.cloned.1.call-update) | async-done | bytes 131088 | tf_op jit(solution)/shard_map/reduce_scatter | solution.py:40
  407.8 1.7 fusion
  (56 shorter events, 2.3 us)
Async XLA Ops:
  6.5 401.3 %copy-start = (bf16[256,256]{1,0:T(8,128)(2,1)S(1)}, bf16[256,256]{1,0:T(8,128)(2,1)}, u32[]{:S(2)}) copy-start(bf16[256,256]{1,0:T(8,128)(2,1)} %param.8) | copy-start | bytes 393220
  6.5 401.3 %reduce-scatter.2.cloned.1.call-start = ((), (), s32[]{:S(2)}) async-start(), calls=%async_computation.2 | async-start | bytes 1179648 | tf_op jit(solution)/shard_map/reduce_scatter | solution.py:40
  44.3 29.5 %collective-permute-start = (bf16[1024,256]{1,0:T(8,128)(2,1)S(1)}, bf16[1024,256]{1,0:T(8,128)(2,1)S(1)}, u32[]{:S(2)}, u32[]{:S(2)}) collective-permute-start(bf16[1024,256]{1,0:T(8,128)(2,1)S(1)} %bitcast.160), channel_id=1, source_target_pairs={{0,64},{8,72},{16,80},{24,88},{32,96},{40,104},{48,112},{56,120},{... | collective-permute-start | bytes 1572872 | tf_op jit(solution)/shard_map/ppermute | solution.py:9
  63.6 42.8 %copy-start.16 = (s32[96,2]{0,1:T(2,128)S(1)}, s32[96,2]{0,1:T(2,128)}, u32[]{:S(2)}) copy-start(s32[96,2]{0,1:T(2,128)} %param.10) | copy-start | bytes 2308
  63.7 42.9 %copy-start.5 = (s32[1,8]{1,0:T(1,128)S(1)}, s32[1,8]{1,0:T(1,128)}, u32[]{:S(2)}) copy-start(s32[1,8]{1,0:T(1,128)} %param.11) | copy-start | bytes 100
  73.9 30.6 %collective-permute-start.1 = (bf16[1024,256]{1,0:T(8,128)(2,1)S(1)}, bf16[1024,256]{1,0:T(8,128)(2,1)S(1)}, u32[]{:S(2)}, u32[]{:S(2)}) collective-permute-start(bf16[1024,256]{1,0:T(8,128)(2,1)S(1)} %broadcast_select_fusion), channel_id=1, source_target_pairs={{0,128},{8,136},{16,144},{24,152},{32,160},{40,168},{48,176},{56,1... | collective-permute-start | bytes 1572872 | tf_op jit(solution)/shard_map/ppermute | solution.py:9
  104.5 45.3 %collective-permute-start.2 = (bf16[1024,256]{1,0:T(8,128)(2,1)S(1)}, bf16[1024,256]{1,0:T(8,128)(2,1)S(1)}, u32[]{:S(2)}, u32[]{:S(2)}) collective-permute-start(bf16[1024,256]{1,0:T(8,128)(2,1)S(1)} %broadcast_select_fusion.1), channel_id=1, source_target_pairs={{0,256},{8,264},{16,272},{24,280},{32,288},{40,296},{48,304},{56,3... | collective-permute-start | bytes 1572872 | tf_op jit(solution)/shard_map/ppermute | solution.py:9
  149.9 10.5 %collective-permute-start.3 = (bf16[1024,256]{1,0:T(8,128)(2,1)S(1)}, bf16[1024,256]{1,0:T(8,128)(2,1)S(1)}, u32[]{:S(2)}, u32[]{:S(2)}) collective-permute-start(bf16[1024,256]{1,0:T(8,128)(2,1)S(1)} %broadcast_select_fusion.2), channel_id=1, source_target_pairs={{0,8},{8,16},{16,24},{24,32},{32,40},{40,48},{48,56},{56,64},{64,7... | collective-permute-start | bytes 1572872 | tf_op jit(solution)/shard_map/ppermute | solution.py:9
  160.4 29.6 %copy-start.2 = (bf16[1024,256]{1,0:T(8,128)(2,1)}, bf16[1024,256]{1,0:T(8,128)(2,1)S(1)}, u32[]{:S(2)}) copy-start(bf16[1024,256]{1,0:T(8,128)(2,1)S(1)} %collective-permute-done.3) | copy-start | bytes 1572868
  160.4 10.5 %collective-permute-start.4 = (bf16[1024,256]{1,0:T(8,128)(2,1)S(1)}, bf16[1024,256]{1,0:T(8,128)(2,1)S(1)}, u32[]{:S(2)}, u32[]{:S(2)}) collective-permute-start(bf16[1024,256]{1,0:T(8,128)(2,1)S(1)} %collective-permute-done.3), channel_id=1, source_target_pairs={{0,8},{8,16},{16,24},{24,32},{32,40},{40,48},{48,56},{56,64},{64,7... | collective-permute-start | bytes 1572872 | tf_op jit(solution)/shard_map/ppermute | solution.py:9
  170.9 15.9 %copy-start.3 = (bf16[1024,256]{1,0:T(8,128)(2,1)}, bf16[1024,256]{1,0:T(8,128)(2,1)S(1)}, u32[]{:S(2)}) copy-start(bf16[1024,256]{1,0:T(8,128)(2,1)S(1)} %collective-permute-done.4) | copy-start | bytes 1572868
  170.9 10.6 %collective-permute-start.5 = (bf16[1024,256]{1,0:T(8,128)(2,1)S(1)}, bf16[1024,256]{1,0:T(8,128)(2,1)}, u32[]{:S(2)}, u32[]{:S(2)}) collective-permute-start(bf16[1024,256]{1,0:T(8,128)(2,1)S(1)} %collective-permute-done.4), channel_id=1, source_target_pairs={{0,8},{8,16},{16,24},{24,32},{32,40},{40,48},{48,56},{56,64},{64,7... | collective-permute-start | bytes 1572872 | tf_op jit(solution)/shard_map/ppermute | solution.py:9
  181.5 14.1 %collective-permute-start.6 = (bf16[1024,256]{1,0:T(8,128)(2,1)}, bf16[1024,256]{1,0:T(8,128)(2,1)}, u32[]{:S(2)}, u32[]{:S(2)}) collective-permute-start(bf16[1024,256]{1,0:T(8,128)(2,1)} %collective-permute-done.5), channel_id=1, source_target_pairs={{0,8},{8,16},{16,24},{24,32},{32,40},{40,48},{48,56},{56,64},{64,7... | collective-permute-start | bytes 1572872 | tf_op jit(solution)/shard_map/ppermute | solution.py:9
  195.7 21.6 %collective-permute-start.7 = (bf16[1024,256]{1,0:T(8,128)(2,1)}, bf16[1024,256]{1,0:T(8,128)(2,1)}, u32[]{:S(2)}, u32[]{:S(2)}) collective-permute-start(bf16[1024,256]{1,0:T(8,128)(2,1)} %collective-permute-done.6), channel_id=1, source_target_pairs={{0,8},{8,16},{16,24},{24,32},{32,40},{40,48},{48,56},{56,64},{64,7... | collective-permute-start | bytes 1572872 | tf_op jit(solution)/shard_map/ppermute | solution.py:9
  203.8 1.6 copy-start.15
  205.4 3.1 copy-start.4
  210.8 1.6 copy-start.14
  217.3 18.3 %collective-permute-start.8 = (bf16[1024,256]{1,0:T(8,128)(2,1)}, bf16[1024,256]{1,0:T(8,128)(2,1)}, u32[]{:S(2)}, u32[]{:S(2)}) collective-permute-start(bf16[1024,256]{1,0:T(8,128)(2,1)} %collective-permute-done.7), channel_id=1, source_target_pairs={{0,8},{8,16},{16,24},{24,32},{32,40},{40,48},{48,56},{56,64},{64,7... | collective-permute-start | bytes 1572872 | tf_op jit(solution)/shard_map/ppermute | solution.py:9
  221.3 1.6 copy-start.13
  229.2 1.6 copy-start.12
  234.0 3.6 copy-start.8
  235.6 16.2 %collective-permute-start.9 = (bf16[1024,256]{1,0:T(8,128)(2,1)}, bf16[1024,256]{1,0:T(8,128)(2,1)}, u32[]{:S(2)}, u32[]{:S(2)}) collective-permute-start(bf16[1024,256]{1,0:T(8,128)(2,1)} %collective-permute-done.8), channel_id=1, source_target_pairs={{0,8},{8,16},{16,24},{24,32},{32,40},{40,48},{48,56},{56,64},{64,7... | collective-permute-start | bytes 1572872 | tf_op jit(solution)/shard_map/ppermute | solution.py:9
  239.1 1.6 copy-start.11
  243.8 1.7 copy-start.7
  243.9 1.7 copy-start.17
  247.0 1.6 copy-start.10
  251.8 1.7 copy-start.6
  251.8 1.7 copy-start.18
  256.1 1.9 copy-start.9
  259.8 1.0 copy-start.1
Sparse Core Ops, SparseCore 0:
  261.0 146.7 reduce-scatter.1
